TPU v7x, 32 devices: a whole 2x2x4 slice. The times are simulated.
32 devices in a mesh: az: 16 (over z, x, core), el: 2 (over y).
Axes of the slice: x: 2, y: 2, z: 4, core: 2. Of those that a mesh axis runs over, the one named last changes fastest.
Arguments:
- raw_sweeps: bfloat16 [4, 1, 24, 96, 256], P('el', None, None, 'az'), may hold values from -6 to 6
- sweep_ids: int32 [4], P('el'), may hold values from 0 to 3, each once
- elevation_embed: float32 [4, 128], replicated, may hold values from -3 to 3
- input_proj: bfloat16 [24, 128], replicated, may hold values from -0.875 to 0.875
- first_kernel: bfloat16 [3, 3, 128, 128], replicated, may hold values from -0.1875 to 0.1875
- second_kernel: bfloat16 [3, 3, 128, 128], replicated, may hold values from -0.1875 to 0.1875
- join_weight: bfloat16 [2, 128, 128], P('el'), may hold values from -0.375 to 0.375
- head_weight: bfloat16 [12, 128], replicated, may hold values from -0.5 to 0.5
- cotangent: bfloat16 [1, 12, 96, 256], P(None, None, 'az'), may hold values from -6 to 6
Outputs:
- prediction: float32 [1, 12, 96, 256], P(None, None, 'az')
- join_grad: float32 [2, 128, 128], P('el')
- first_kernel_gradient: float32 [3, 3, 128, 128], replicated
- second_kernel_gradient: float32 [3, 3, 128, 128], replicated
- input_grad: float32 [24, 128], replicated
- embed_grad: float32 [4, 128], replicated
Inputs may be any that keep to these rules, and one draw needn't show every extreme that they name: `sweep_ids`: each sweep fills exactly one slot.
All inputs are finite; a program needn't handle non-finite values.
Results may differ from a plain program's by a relative error of at most 0.023.
Values may be sent and summed in bfloat16 or wider, within the bound.
A program may use at most 64 MiB of HBM per device.

v0:
```python
import math
import jax
import jax.numpy as jnp
from jax import lax
from jax.sharding import PartitionSpec as P

CHANNELS = 128
FIRST_DILATION = 1
SECOND_DILATION = 2
precise = lax.Precision.HIGHEST


def padded_2(block, sides, width):
    for axis, dim in sides:
        count = lax.axis_size(axis)
        forward = [(i, i + 1) for i in range(count - 1)]
        forward.append((count - 1, 0))
        backward = [(target, source) for source, target in forward]
        low = lax.ppermute(
            lax.slice_in_dim(block, block.shape[dim] - width, None, axis=dim), axis, forward
        )
        high = lax.ppermute(lax.slice_in_dim(block, 0, width, axis=dim), axis, backward)
        block = jnp.concatenate([low, block, high], axis=dim)
    return block


def silu_slope(values):
    logistic = jax.nn.sigmoid(values)
    return logistic * (1.0 + values * (1.0 - logistic))


def range_padding(source, dilate):
    return jnp.pad(source, ((0, 0), (0, 0), (0, 0), (dilate, dilate)))


def convolve_partial(padded, kernel, dilate):
    return lax.conv_general_dilated(
        padded,
        kernel,
        (1, 1),
        "VALID",
        rhs_dilation=(dilate, dilate),
        dimension_numbers=("NCHW", "HWIO", "NCHW"),
        preferred_element_type=jnp.float32,
    )


def reversed_kernel(kernel):
    return jnp.flip(kernel, (0, 1)).transpose(0, 1, 3, 2)


def kernel_gradient_of(padded, upstream, dilate):
    ray_count = upstream.shape[2]
    gate_count = upstream.shape[3]
    tap_rows = []
    for tap_row in range(3):
        tap_line = []
        for tap_column in range(3):
            window = padded[
                :,
                :,
                tap_row * dilate : tap_row * dilate + ray_count,
                tap_column * dilate : tap_column * dilate + gate_count,
            ]
            tap_line.append(
                jnp.einsum("niar,noar->io", window, upstream, preferred_element_type=jnp.float32)
            )
        tap_rows.append(jnp.stack(tap_line))
    return jnp.stack(tap_rows)


def activate(source):
    return jax.nn.silu(source.astype(jnp.float32)).astype(jnp.bfloat16)


def shards(
    raw_sweeps,
    sweep_ids,
    elevation_embed,
    input_proj,
    first_kernel,
    second_kernel,
    join_weight,
    head_weight,
    cotangent,
):
    brain_float_half = jnp.bfloat16
    sweep_total = elevation_embed.shape[0]
    onehot = (sweep_ids[:, None] == jnp.arange(sweep_total, dtype=jnp.int32)[None, :]).astype(
        jnp.float32
    )
    bias_rows = jnp.dot(onehot, elevation_embed, precision=precise)
    group_bias = jnp.sum(bias_rows, axis=0)
    input_state = jnp.einsum(
        "jbiar,ic->bcar", raw_sweeps, input_proj, preferred_element_type=jnp.float32
    )
    input_state = (input_state + group_bias[None, :, None, None]).astype(brain_float_half)
    input_activation = activate(input_state)
    padded_input = range_padding(
        padded_2(input_activation, (("az", 2),), FIRST_DILATION), FIRST_DILATION
    )
    hidden_state = (
        input_state.astype(jnp.float32)
        + convolve_partial(padded_input, first_kernel, FIRST_DILATION)
    ).astype(brain_float_half)
    hidden_activation = activate(hidden_state)
    padded_hidden = range_padding(
        padded_2(hidden_activation, (("az", 2),), SECOND_DILATION), SECOND_DILATION
    )
    final_state = (
        hidden_state.astype(jnp.float32)
        + convolve_partial(padded_hidden, second_kernel, SECOND_DILATION)
    ).astype(brain_float_half)
    group_weight = join_weight[0]
    empty_sum = jnp.zeros((CHANNELS,) + final_state.shape[:1] + final_state.shape[2:], jnp.float32)
    joined_all = (
        empty_sum
        + jnp.einsum(
            "gbiar,gio->obar",
            lax.all_gather(final_state[None], "el", axis=0, tiled=True),
            lax.all_gather(join_weight, "el", axis=0, tiled=True),
            preferred_element_type=jnp.float32,
        )
    ).astype(brain_float_half)
    prediction = jnp.einsum(
        "lc,cbar->blar", head_weight, joined_all, preferred_element_type=jnp.float32
    )
    ray_total = final_state.shape[2] * lax.axis_size("az")
    grad_scale = 1.0 / math.sqrt(
        lax.axis_size("el") * final_state.shape[0] * ray_total * final_state.shape[3]
    )
    joined_back = jnp.einsum(
        "lc,blar->bcar", head_weight, cotangent, preferred_element_type=jnp.float32
    ).astype(brain_float_half)
    join_local = jnp.einsum(
        "biar,boar->io", final_state, joined_back, preferred_element_type=jnp.float32
    )
    join_total = lax.psum(join_local, "az")
    grad_two = jnp.einsum(
        "io,boar->biar", group_weight, joined_back, preferred_element_type=jnp.float32
    )
    final_upstream_gradient = grad_two.astype(brain_float_half)
    second_kernel_partial = kernel_gradient_of(
        padded_hidden, final_upstream_gradient, SECOND_DILATION
    )
    second_border_rays = range_padding(
        padded_2(final_upstream_gradient, (("az", 2),), SECOND_DILATION), SECOND_DILATION
    )
    second_backward_pass = convolve_partial(
        second_border_rays, reversed_kernel(second_kernel), SECOND_DILATION
    )
    grad_one = grad_two + second_backward_pass * silu_slope(hidden_state.astype(jnp.float32))
    hidden_upstream_gradient = grad_one.astype(brain_float_half)
    first_kernel_partial = kernel_gradient_of(
        padded_input, hidden_upstream_gradient, FIRST_DILATION
    )
    first_border_rays = range_padding(
        padded_2(hidden_upstream_gradient, (("az", 2),), FIRST_DILATION), FIRST_DILATION
    )
    first_backward_pass = convolve_partial(
        first_border_rays, reversed_kernel(first_kernel), FIRST_DILATION
    )
    grad_zero = (
        grad_one + first_backward_pass * silu_slope(input_state.astype(jnp.float32))
    ).astype(brain_float_half)
    input_local = jnp.einsum(
        "jbiar,bcar->ic", raw_sweeps, grad_zero, preferred_element_type=jnp.float32
    )
    column_sum = jnp.sum(grad_zero.astype(jnp.float32), axis=(0, 2, 3))
    slot_terms = jnp.broadcast_to(column_sum[None, :], (raw_sweeps.shape[0], column_sum.shape[0]))
    embed_local = jnp.dot(onehot.T, slot_terms, precision=precise)
    second_total, first_total, input_total, embed_total = lax.psum(
        (second_kernel_partial, first_kernel_partial, input_local, embed_local), ("az", "el")
    )
    return (
        prediction,
        join_total[None] * grad_scale,
        first_total * grad_scale,
        second_total * grad_scale,
        input_total * grad_scale,
        embed_total * grad_scale,
    )


def solution(mesh):
    in_specs = (
        P("el", None, None, "az", None),
        P("el"),
        P(),
        P(),
        P(),
        P(),
        P("el", None, None),
        P(),
        P(None, None, "az", None),
    )
    out_specs = (P(None, None, "az", None), P("el", None, None), P(), P(), P(), P())
    return jax.shard_map(shards, mesh=mesh, in_specs=in_specs, out_specs=out_specs, check_vma=False)
```

profile of v0, /device:TPU:0, one launch (start us, length us, event | category | flops | bytes accessed | tf_op | source)
XLA Modules:
  0.0 342.1 jit_solution(14312674388534561637)
XLA Ops:
  7.2 1.0 convert_reduce_fusion.1
  8.2 0.9 convolution_reduce_fusion
  9.1 1.9 fusion.30
  11.1 0.5 collective-permute-start
  11.6 5.0 %collective-permute-start.1 = (bf16[1,128,1,256]{1,3,2,0:T(8,128)(2,1)S(1)}, bf16[1,128,1,256]{1,3,2,0:T(8,128)(2,1)S(1)}, u32[]{:S(2)}, u32[]{:S(2)}) collective-permute-start(bf16[1,128,1,256]{1,3,2,0:T(8,128)(2,1)S(1)} %get-tuple-element.42), channel_id=1, source_target_pairs={{2,0},{4,2},{6,4},{8,6},{10,8},{12,10},{14,12},{16,14},{18,16},{20... | collective-permute-start | bytes 196616 | tf_op jit(solution)/shard_map/ppermute | solution.py:22
  16.9 1.2 fusion.177
  18.2 4.4 %collective-permute-start.5 = (bf16[1,128,2,256]{1,3,2,0:T(8,128)(2,1)S(1)}, bf16[1,128,2,256]{1,3,2,0:T(8,128)(2,1)S(1)}, u32[]{:S(2)}, u32[]{:S(2)}) collective-permute-start(bf16[1,128,2,256]{1,3,2,0:T(8,128)(2,1)S(1)} %get-tuple-element.44), channel_id=1, source_target_pairs={{2,0},{4,2},{6,4},{8,6},{10,8},{12,10},{14,12},{16,14},{18,16},{20... | collective-permute-start | bytes 393224 | tf_op jit(solution)/shard_map/ppermute | solution.py:22
  22.6 4.7 %all_gather.7 = bf16[2,128,128]{2,1,0:T(8,128)(2,1)} all-gather(bf16[1,128,128]{2,1,0:T(8,128)(2,1)S(1)} %copy-done.10), channel_id=1, replica_groups=mesh['az'=16,'el'=2] {'el'}, dimensions={0}, use_global_device_ids=true | all-gather | bytes 98304 | tf_op jit(solution)/shard_map/all_gather | solution.py:121
  27.4 0.3 copy.223
  28.1 0.5 copy-done.22
  28.6 1.1 convolution_select_fusion.3
  29.9 1.0 reshape.182
  31.5 0.8 copy-done.19
  32.4 1.1 convolution_select_fusion.1
  33.7 1.0 reshape.186
  34.6 3.1 fusion.170
  38.0 0.9 convolution_bitcast_fusion.6
  40.2 0.4 copy-done.2
  40.5 0.3 convolution_bitcast_fusion.15
  41.6 4.4 %collective-permute-start.7 = (bf16[1,128,1,256]{1,3,2,0:T(8,128)(2,1)S(1)}, bf16[1,128,1,256]{1,3,2,0:T(8,128)(2,1)S(1)}, u32[]{:S(2)}, u32[]{:S(2)}) collective-permute-start(bf16[1,128,1,256]{1,3,2,0:T(8,128)(2,1)S(1)} %get-tuple-element.38), channel_id=1, source_target_pairs={{2,0},{4,2},{6,4},{8,6},{10,8},{12,10},{14,12},{16,14},{18,16},{20... | collective-permute-start | bytes 196616 | tf_op jit(solution)/shard_map/ppermute | solution.py:22
  46.0 4.4 %collective-permute-start.3 = (bf16[1,128,2,256]{1,3,2,0:T(8,128)(2,1)S(1)}, bf16[1,128,2,256]{1,3,2,0:T(8,128)(2,1)S(1)}, u32[]{:S(2)}, u32[]{:S(2)}) collective-permute-start(bf16[1,128,2,256]{1,3,2,0:T(8,128)(2,1)S(1)} %get-tuple-element.40), channel_id=1, source_target_pairs={{2,0},{4,2},{6,4},{8,6},{10,8},{12,10},{14,12},{16,14},{18,16},{20... | collective-permute-start | bytes 393224 | tf_op jit(solution)/shard_map/ppermute | solution.py:22
  51.1 0.9 pad_maximum_fusion.1
  52.1 0.3 copy.224
  52.6 1.1 convolution_select_fusion
  53.9 1.0 reshape.188
  54.8 2.0 convert_reduce_fusion
  57.2 37.2 %all-reduce.2 = (f32[24,128]{1,0:T(8,128)S(1)}, f32[4,128]{1,0:T(4,128)S(1)}) all-reduce(f32[24,128]{1,0:T(8,128)S(1)} %convolution_bitcast_fusion.21, f32[4,128]{1,0:T(4,128)S(1)} %fusion.135), channel_id=1, replica_groups=mesh['az'=16,'el'=2] {'az','el'}, use_global_device_ids=true, to_apply=%region_5.6 | all-reduce | flops 3584 | bytes 28672 | tf_op jit(solution)/shard_map/psum | solution.py:172
  94.5 0.6 broadcast_multiply_fusion.2
  95.2 0.5 copy-done.11
  96.4 0.9 convolution_bitcast_fusion.7
  97.3 0.9 convolution_bitcast_fusion.8
  98.3 0.9 convolution_bitcast_fusion.2
  99.2 0.9 convolution_bitcast_fusion.4
  100.7 0.8 copy-done.20
  101.5 1.1 convolution_select_fusion.2
  102.8 1.0 reshape.184
  103.8 1.2 fusion.15
  105.1 0.9 convolution_bitcast_fusion.20
  107.0 0.9 pad_maximum_fusion.2
  107.9 0.6 broadcast_multiply_fusion.3
  108.6 11.7 %all-gather = bf16[2,128,6,256]{3,1,2,0:T(8,128)(2,1)S(1)} all-gather(bf16[1,128,6,256]{3,1,2,0:T(8,128)(2,1)S(1)} %copy.130), channel_id=2, replica_groups=mesh['az'=16,'el'=2] {'el'}, dimensions={0}, use_global_device_ids=true | all-gather | bytes 1179648 | tf_op jit(solution)/shard_map/all_gather | solution.py:120
  120.3 0.7 fusion.10
  121.0 0.7 copy.180
  121.8 70.7 %all-reduce.7.cloned.1.call-done = f32[128,128]{1,0:T(8,128)} async-done(((f32[128,128]{1,0:T(8,128)}), f32[128,128]{1,0:T(8,128)}) %all-reduce.7.cloned.1.call-update) | async-done | bytes 65552 | tf_op jit(solution)/shard_map/psum | solution.py:138
  192.5 1.5 multiply_bitcast_fusion
  193.9 138.5 %all-reduce.9.cloned.1.call-done = (f32[3,3,128,128]{3,2,1,0:T(8,128)}, f32[3,3,128,128]{3,2,1,0:T(8,128)}) async-done(((f32[3,3,128,128]{3,2,1,0:T(8,128)}, f32[3,3,128,128]{3,2,1,0:T(8,128)}), (f32[3,3,128,128]{3,2,1,0:T(8,128)}, f32[3,3,128,128]{3,2,1,0:T(8,128)})) %all-reduce.9.cloned.1.call-update) | async-done | bytes 1179664 | tf_op jit(solution)/shard_map/psum | solution.py:172
  332.4 2.0 broadcast_multiply_fusion
  334.4 0.9 broadcast_multiply_fusion.1
  (103 shorter events, 7.9 us)
Async XLA Ops:
  7.2 20.9 %copy-start = (bf16[3,3,128,128]{3,2,1,0:T(8,128)(2,1)S(1)}, bf16[3,3,128,128]{3,2,1,0:T(8,128)(2,1)}, u32[]{:S(2)}) copy-start(bf16[3,3,128,128]{3,2,1,0:T(8,128)(2,1)} %param.13) | copy-start | bytes 884740
  7.2 185.3 %all-reduce.7.cloned.1.call-start = ((), (), s32[]{:S(2)}) async-start(), calls=%async_computation | async-start | bytes 131072 | tf_op jit(solution)/shard_map/psum | solution.py:138
  9.1 7.5 %copy-start.17 = (bf16[1,12,6,256]{3,2,1,0:T(8,128)(2,1)S(1)}, bf16[1,12,6,256]{3,2,1,0:T(8,128)(2,1)}, u32[]{:S(2)}) copy-start(bf16[1,12,6,256]{3,2,1,0:T(8,128)(2,1)} %param.17) | copy-start | bytes 110596
  9.1 7.5 %copy-start.18 = (bf16[12,128]{1,0:T(8,128)(2,1)S(1)}, bf16[12,128]{1,0:T(8,128)(2,1)}, u32[]{:S(2)}) copy-start(bf16[12,128]{1,0:T(8,128)(2,1)} %param.16) | copy-start | bytes 9220
  9.1 7.8 %copy-start.10 = (bf16[1,128,128]{2,1,0:T(8,128)(2,1)S(1)}, bf16[1,128,128]{2,1,0:T(8,128)(2,1)}, u32[]{:S(2)}) copy-start(bf16[1,128,128]{2,1,0:T(8,128)(2,1)} %param.15) | copy-start | bytes 98308
  11.1 16.2 %copy-start.1 = (bf16[128,6,256]{0,2,1:T(8,128)(2,1)}, bf16[128,6,256]{0,2,1:T(8,128)(2,1)S(1)}, u32[]{:S(2)}) copy-start(bf16[128,6,256]{0,2,1:T(8,128)(2,1)S(1)} %get-tuple-element.47) | copy-start | bytes 1179652
  11.1 16.2 %collective-permute-start = (bf16[1,128,1,256]{1,3,2,0:T(8,128)(2,1)S(1)}, bf16[1,128,1,256]{1,3,2,0:T(8,128)(2,1)S(1)}, u32[]{:S(2)}, u32[]{:S(2)}) collective-permute-start(bf16[1,128,1,256]{1,3,2,0:T(8,128)(2,1)S(1)} %get-tuple-element.41), channel_id=1, source_target_pairs={{0,2},{2,4},{4,6},{6,8},{8,10},{10,12},{12,14},{14,16},{16,18},{18... | collective-permute-start | bytes 196616 | tf_op jit(solution)/shard_map/ppermute | solution.py:19
  11.6 15.7 %collective-permute-start.1 = (bf16[1,128,1,256]{1,3,2,0:T(8,128)(2,1)S(1)}, bf16[1,128,1,256]{1,3,2,0:T(8,128)(2,1)S(1)}, u32[]{:S(2)}, u32[]{:S(2)}) collective-permute-start(bf16[1,128,1,256]{1,3,2,0:T(8,128)(2,1)S(1)} %get-tuple-element.42), channel_id=1, source_target_pairs={{2,0},{4,2},{6,4},{8,6},{10,8},{12,10},{14,12},{16,14},{18,16},{20... | collective-permute-start | bytes 196616 | tf_op jit(solution)/shard_map/ppermute | solution.py:22
  18.1 12.8 %collective-permute-start.4 = (bf16[1,128,2,256]{1,3,2,0:T(8,128)(2,1)S(1)}, bf16[1,128,2,256]{1,3,2,0:T(8,128)(2,1)S(1)}, u32[]{:S(2)}, u32[]{:S(2)}) collective-permute-start(bf16[1,128,2,256]{1,3,2,0:T(8,128)(2,1)S(1)} %get-tuple-element.43), channel_id=1, source_target_pairs={{0,2},{2,4},{4,6},{6,8},{8,10},{10,12},{12,14},{14,16},{16,18},{18... | collective-permute-start | bytes 393224 | tf_op jit(solution)/shard_map/ppermute | solution.py:19
  18.2 12.7 %collective-permute-start.5 = (bf16[1,128,2,256]{1,3,2,0:T(8,128)(2,1)S(1)}, bf16[1,128,2,256]{1,3,2,0:T(8,128)(2,1)S(1)}, u32[]{:S(2)}, u32[]{:S(2)}) collective-permute-start(bf16[1,128,2,256]{1,3,2,0:T(8,128)(2,1)S(1)} %get-tuple-element.44), channel_id=1, source_target_pairs={{2,0},{4,2},{6,4},{8,6},{10,8},{12,10},{14,12},{16,14},{18,16},{20... | collective-permute-start | bytes 393224 | tf_op jit(solution)/shard_map/ppermute | solution.py:22
  27.3 0.6 copy-start.15
  27.9 0.7 copy-start.22
  31.4 1.0 copy-start.19
  39.5 1.0 copy-start.2
  40.9 9.6 %copy-start.16 = (bf16[1,128,1,256]{1,3,2,0:T(8,128)(2,1)S(1)}, bf16[1,128,1,256]{1,3,2,0:T(8,128)(2,1)}, u32[]{:S(2)}) copy-start(bf16[1,128,1,256]{1,3,2,0:T(8,128)(2,1)} %copy-done.15) | copy-start | bytes 196612
  41.5 10.5 %collective-permute-start.6 = (bf16[1,128,1,256]{1,3,2,0:T(8,128)(2,1)S(1)}, bf16[1,128,1,256]{1,3,2,0:T(8,128)(2,1)S(1)}, u32[]{:S(2)}, u32[]{:S(2)}) collective-permute-start(bf16[1,128,1,256]{1,3,2,0:T(8,128)(2,1)S(1)} %get-tuple-element.37), channel_id=1, source_target_pairs={{0,2},{2,4},{4,6},{6,8},{8,10},{10,12},{12,14},{14,16},{16,18},{18... | collective-permute-start | bytes 196616 | tf_op jit(solution)/shard_map/ppermute | solution.py:19
  41.6 10.4 %collective-permute-start.7 = (bf16[1,128,1,256]{1,3,2,0:T(8,128)(2,1)S(1)}, bf16[1,128,1,256]{1,3,2,0:T(8,128)(2,1)S(1)}, u32[]{:S(2)}, u32[]{:S(2)}) collective-permute-start(bf16[1,128,1,256]{1,3,2,0:T(8,128)(2,1)S(1)} %get-tuple-element.38), channel_id=1, source_target_pairs={{2,0},{4,2},{6,4},{8,6},{10,8},{12,10},{14,12},{16,14},{18,16},{20... | collective-permute-start | bytes 196616 | tf_op jit(solution)/shard_map/ppermute | solution.py:22
  46.0 49.1 %collective-permute-start.2 = (bf16[1,128,2,256]{1,3,2,0:T(8,128)(2,1)S(1)}, bf16[1,128,2,256]{1,3,2,0:T(8,128)(2,1)S(1)}, u32[]{:S(2)}, u32[]{:S(2)}) collective-permute-start(bf16[1,128,2,256]{1,3,2,0:T(8,128)(2,1)S(1)} %get-tuple-element.39), channel_id=1, source_target_pairs={{0,2},{2,4},{4,6},{6,8},{8,10},{10,12},{12,14},{14,16},{16,18},{18... | collective-permute-start | bytes 393224 | tf_op jit(solution)/shard_map/ppermute | solution.py:19
  46.0 49.1 %collective-permute-start.3 = (bf16[1,128,2,256]{1,3,2,0:T(8,128)(2,1)S(1)}, bf16[1,128,2,256]{1,3,2,0:T(8,128)(2,1)S(1)}, u32[]{:S(2)}, u32[]{:S(2)}) collective-permute-start(bf16[1,128,2,256]{1,3,2,0:T(8,128)(2,1)S(1)} %get-tuple-element.40), channel_id=1, source_target_pairs={{2,0},{4,2},{6,4},{8,6},{10,8},{12,10},{14,12},{16,14},{18,16},{20... | collective-permute-start | bytes 393224 | tf_op jit(solution)/shard_map/ppermute | solution.py:22
  54.8 2.2 copy-start.21
  95.1 0.7 copy-start.11
  95.1 0.7 copy-start.13
  100.6 1.0 copy-start.20
  103.8 2.3 copy-start.14
  105.1 1.4 copy-start.6
  105.1 1.4 copy-start.7
  105.1 1.4 copy-start.12
  106.0 0.8 copy-start.4
  106.1 0.9 copy-start.5
  106.1 0.9 copy-start.8
  106.1 226.3 %all-reduce.9.cloned.1.call-start = ((), (), s32[]{:S(2)}) async-start(), calls=%async_computation.1 | async-start | bytes 2359296 | tf_op jit(solution)/shard_map/psum | solution.py:172
  108.5 11.9 %copy-start.9 = (bf16[2,128,128]{2,1,0:T(8,128)(2,1)S(1)}, bf16[2,128,128]{2,1,0:T(8,128)(2,1)}, u32[]{:S(2)}) copy-start(bf16[2,128,128]{2,1,0:T(8,128)(2,1)} %all_gather.7) | copy-start | bytes 196612
  332.4 2.0 copy-start.3
Sparse Core Ops, SparseCore 0:
  106.2 86.2 all-reduce.6
  199.5 132.8 all-reduce.8
where the time goes:
time: 343 us; the launch traced here: 342 us
  waiting for transfers between devices  209 us (61%)
  blocking collectives  53.6 us (16%)
  matrix products  19.5 us (6%)
  starting transfers between devices  19 us (6%)
  other arithmetic  15.1 us (4%)
  between operations  14.6 us (4%)
  local copies, waits for them, and re-layouts  11 us (3%)
    psum x1, waiting for transfers between devices, shards(): lax.psum((second_kernel_partial, first_kernel_partial, input_local, embed...  138 us
    psum x1, waiting for transfers between devices, shards(): join_total = lax.psum(join_local, 'az')  70.7 us
    psum x1, blocking collectives, shards(): lax.psum((second_kernel_partial, first_kernel_partial, input_local, embed...  37.2 us
    ppermute x4, starting transfers between devices, padded_2(): lax.ppermute(lax.slice_in_dim(block, 0, width, axis=dim), axis, backward)  18.3 us
    all_gather x1, blocking collectives, shards(): lax.all_gather(final_state[None], 'el', axis=0, tiled=True)  11.7 us
    dot_general x18, matrix products, kernel_gradient_of(): jnp.einsum('niar,noar->io', window, upstream, preferred_element_type=jnp....  8.68 us
  transfers between devices with their start and end apart: 10, of which 2 were waited for; matrix products, arithmetic and copies ran while one was open for 5% of the time, Pallas kernels for 0%

commit v1 on v0

--- a/solution.py
+++ b/solution.py
@@ -170,7 +170,8 @@
     slot_terms = jnp.broadcast_to(column_sum[None, :], (raw_sweeps.shape[0], column_sum.shape[0]))
     embed_local = jnp.dot(onehot.T, slot_terms, precision=precise)
     second_total, first_total, input_total, embed_total = lax.psum(
-        (second_kernel_partial, first_kernel_partial, input_local, embed_local), ("az", "el")
+        lax.psum((second_kernel_partial, first_kernel_partial, input_local, embed_local), "el"),
+        "az",
     )
     return (
         prediction,

time: 343 us -> 237 us (0.69)
  waiting for transfers between devices: 209 us -> 79.5 us
  blocking collectives: 53.6 us -> 80 us
    psum x1, waiting for transfers between devices: 138 us -> 0.01 us  [shards(): lax.psum((second_kernel_partial, first_kernel_partial, input_local, embed...]
    psum x0 -> x1, blocking collectives: none -> 58.2 us  [shards(): lax.psum(lax.psum((second_kernel_partial, first_kernel_partial, input_loc...]
    psum x1, blocking collectives: 37.2 us -> 8.67 us  [shards(): lax.psum((second_kernel_partial, first_kernel_partial, input_local, embed...]
    psum x1, waiting for transfers between devices: 70.7 us -> 79.4 us  [shards(): join_total = lax.psum(join_local, 'az')]
  transfers between devices with their start and end apart: 10 -> 10, of which waited for: 2 -> 1; matrix products, arithmetic and copies ran while one was open for 5% -> 7% of each run, Pallas kernels for 0% -> 0%
where the time goes in v1:
time: 237 us
  blocking collectives  80 us (34%)
  waiting for transfers between devices  79.5 us (34%)
  starting transfers between devices  19 us (8%)
  matrix products  17.1 us (7%)
  between operations  14.5 us (6%)
  local copies, waits for them, and re-layouts  14.2 us (6%)
  other arithmetic  12.4 us (5%)
    psum x1, waiting for transfers between devices, shards(): join_total = lax.psum(join_local, 'az')  79.4 us
    psum x1, blocking collectives, shards(): lax.psum(lax.psum((second_kernel_partial, first_kernel_partial, input_loc...  58.2 us
    ppermute x4, starting transfers between devices, padded_2(): lax.ppermute(lax.slice_in_dim(block, 0, width, axis=dim), axis, backward)  18.3 us
    psum x1, blocking collectives, shards(): lax.psum((second_kernel_partial, first_kernel_partial, input_local, embed...  8.67 us
    all_gather x1, blocking collectives, shards(): lax.all_gather(final_state[None], 'el', axis=0, tiled=True)  8.45 us
    dot_general x18, matrix products, kernel_gradient_of(): jnp.einsum('niar,noar->io', window, upstream, preferred_element_type=jnp....  6.18 us
    conv_general_dilated x18, local copies, waits for them, and re-layouts, convolve_partial(): lax.conv_general_dilated(padded, kernel, (1, 1), 'VALID', rhs_dilation=(d...  5.56 us
    unnamed x41, local copies, waits for them, and re-layouts  5.37 us
  transfers between devices with their start and end apart: 10, of which 1 were waited for; matrix products, arithmetic and copies ran while one was open for 7% of the time, Pallas kernels for 0%

profile of v1, /device:TPU:0, one launch (start us, length us, event | category | flops | bytes accessed | tf_op | source)
XLA Modules:
  0.0 236.6 jit_solution(4627080914017092833)
XLA Ops:
  7.2 1.0 convert_reduce_fusion.1
  8.2 0.9 convolution_reduce_fusion
  9.1 1.9 fusion.30
  11.1 0.5 collective-permute-start
  11.6 5.0 %collective-permute-start.1 = (bf16[1,128,1,256]{1,3,2,0:T(8,128)(2,1)S(1)}, bf16[1,128,1,256]{1,3,2,0:T(8,128)(2,1)S(1)}, u32[]{:S(2)}, u32[]{:S(2)}) collective-permute-start(bf16[1,128,1,256]{1,3,2,0:T(8,128)(2,1)S(1)} %get-tuple-element.47), channel_id=1, source_target_pairs={{2,0},{4,2},{6,4},{8,6},{10,8},{12,10},{14,12},{16,14},{18,16},{20... | collective-permute-start | bytes 196616 | tf_op jit(solution)/shard_map/ppermute | solution.py:22
  16.9 1.2 fusion.177
  18.1 0.7 fusion.176
  18.9 4.4 %collective-permute-start.5 = (bf16[1,128,2,256]{1,3,2,0:T(8,128)(2,1)}, bf16[1,128,2,256]{1,3,2,0:T(8,128)(2,1)S(1)}, u32[]{:S(2)}, u32[]{:S(2)}) collective-permute-start(bf16[1,128,2,256]{1,3,2,0:T(8,128)(2,1)} %get-tuple-element.49), channel_id=1, source_target_pairs={{2,0},{4,2},{6,4},{8,6},{10,8},{12,10},{14,12},{16,14},{18,16},{20... | collective-permute-start | bytes 393224 | tf_op jit(solution)/shard_map/ppermute | solution.py:22
  23.3 4.7 %all_gather.7 = bf16[2,128,128]{2,1,0:T(8,128)(2,1)} all-gather(bf16[1,128,128]{2,1,0:T(8,128)(2,1)S(1)} %copy-done.9), channel_id=1, replica_groups=mesh['az'=16,'el'=2] {'el'}, dimensions={0}, use_global_device_ids=true | all-gather | bytes 98304 | tf_op jit(solution)/shard_map/all_gather | solution.py:121
  28.1 0.3 copy.223
  28.8 0.5 copy-done.18
  29.3 1.1 convolution_select_fusion.3
  30.6 1.0 reshape.182
  31.7 1.0 pad.16
  32.7 1.3 reshape.173
  34.2 0.8 copy-done.15
  35.0 1.1 convolution_select_fusion.1
  36.3 1.0 reshape.186
  37.3 3.1 %fusion.170 = (bf16[1,128,6,256]{1,3,2,0:T(8,128)(2,1)S(1)}, f32[1,128,6,256]{1,3,2,0:T(8,128)}, bf16[1,128,6,256]{1,3,2,0:T(8,128)(2,1)S(1)}) fusion(f32[1,128,6,256]{1,3,2,0:T(8,128)} %get-tuple-element.51, f32[6,1,264,128]{3,2,0,1:T(8,128)} %reshape.186, f32[6,1,264,128]{3,2,0,1:T(8,128)} %reshape.182, f32[6,256,128]{2,1,0:T(8,128)} %get-tuple-element.53), kind=kLoop, calls=%fused_computation.226 | loop fusion | flops 2555904 | bytes 4718592 | tf_op jit(solution)/shard_map/convert_element_type | solution.py:153
  40.6 0.9 convolution_bitcast_fusion.6
  42.8 0.4 copy-done.5
  43.2 0.3 convolution_bitcast_fusion.15
  44.2 4.4 %collective-permute-start.7 = (bf16[1,128,1,256]{1,3,2,0:T(8,128)(2,1)S(1)}, bf16[1,128,1,256]{1,3,2,0:T(8,128)(2,1)S(1)}, u32[]{:S(2)}, u32[]{:S(2)}) collective-permute-start(bf16[1,128,1,256]{1,3,2,0:T(8,128)(2,1)S(1)} %get-tuple-element.43), channel_id=1, source_target_pairs={{2,0},{4,2},{6,4},{8,6},{10,8},{12,10},{14,12},{16,14},{18,16},{20... | collective-permute-start | bytes 196616 | tf_op jit(solution)/shard_map/ppermute | solution.py:22
  48.6 4.4 %collective-permute-start.3 = (bf16[1,128,2,256]{1,3,2,0:T(8,128)(2,1)S(1)}, bf16[1,128,2,256]{1,3,2,0:T(8,128)(2,1)S(1)}, u32[]{:S(2)}, u32[]{:S(2)}) collective-permute-start(bf16[1,128,2,256]{1,3,2,0:T(8,128)(2,1)S(1)} %get-tuple-element.45), channel_id=1, source_target_pairs={{2,0},{4,2},{6,4},{8,6},{10,8},{12,10},{14,12},{16,14},{18,16},{20... | collective-permute-start | bytes 393224 | tf_op jit(solution)/shard_map/ppermute | solution.py:22
  53.8 0.9 pad_maximum_fusion.1
  54.7 0.3 copy.224
  55.2 1.1 convolution_select_fusion
  56.5 1.0 reshape.188
  57.5 0.9 pad_maximum_fusion
  59.7 0.3 convolution_bitcast_fusion.2
  61.2 0.9 pad_maximum_fusion.2
  62.1 0.4 copy-done.3
  63.0 0.4 convert_reduce_fusion
  63.9 8.7 %all-reduce.4 = (f32[24,128]{1,0:T(8,128)S(1)}, f32[4,128]{1,0:T(4,128)S(1)}) all-reduce(f32[24,128]{1,0:T(8,128)S(1)} %convolution_bitcast_fusion.21, f32[4,128]{1,0:T(4,128)S(1)} %fusion.135), channel_id=1, replica_groups=mesh['az'=16,'el'=2] {'el'}, use_global_device_ids=true, to_apply=%region_7.8 | all-reduce | flops 3584 | bytes 28672 | tf_op jit(solution)/shard_map/psum | solution.py:173
  72.5 58.2 %all-reduce.2 = (f32[24,128]{1,0:T(8,128)S(1)}, f32[4,128]{1,0:T(4,128)S(1)}) all-reduce(f32[24,128]{1,0:T(8,128)S(1)} %get-tuple-element.29, f32[4,128]{1,0:T(4,128)S(1)} %get-tuple-element.30), channel_id=1, replica_groups=mesh['az'=16,'el'=2] {'az'}, use_global_device_ids=true, to_apply=%region_8.9 | all-reduce | flops 3584 | bytes 28672 | tf_op jit(solution)/shard_map/psum | solution.py:172
  130.7 1.3 pad.14
  132.4 0.8 copy-done.16
  133.2 1.1 convolution_select_fusion.2
  134.7 0.9 convolution_bitcast_fusion.20
  135.6 0.6 broadcast_multiply_fusion.3
  136.2 0.6 broadcast_multiply_fusion.2
  137.0 8.5 %all-gather = bf16[2,128,6,256]{3,1,2,0:T(8,128)(2,1)S(1)} all-gather(bf16[1,128,6,256]{3,1,2,0:T(8,128)(2,1)S(1)} %copy.130), channel_id=2, replica_groups=mesh['az'=16,'el'=2] {'el'}, dimensions={0}, use_global_device_ids=true | all-gather | bytes 1179648 | tf_op jit(solution)/shard_map/all_gather | solution.py:120
  145.5 0.7 fusion.10
  146.1 0.7 copy.180
  146.9 79.4 %all-reduce.9.cloned.1.call-done = (f32[128,128]{1,0:T(8,128)}, f32[3,3,128,128]{3,2,1,0:T(8,128)}, f32[3,3,128,128]{3,2,1,0:T(8,128)}) async-done(((f32[128,128]{1,0:T(8,128)}, f32[3,3,128,128]{3,2,1,0:T(8,128)}, f32[3,3,128,128]{3,2,1,0:T(8,128)}), (f32[128,128]{1,0:T(8,128)}, f32[3,3,128,128]{3,2,1,0:T(8,128)}, f32[3,3,128,128]{3,2,1,0:T(8,128)})) %all-reduce.9.cloned.1.call-update) | async-done | bytes 1245200 | tf_op jit(solution)/shard_map/psum | solution.py:138
  226.3 2.0 broadcast_multiply_fusion
  228.3 0.9 broadcast_multiply_fusion.1
  229.2 0.6 multiply_bitcast_fusion
  (96 shorter events, 8.8 us)
Async XLA Ops:
  7.2 21.6 %copy-start = (bf16[3,3,128,128]{3,2,1,0:T(8,128)(2,1)S(1)}, bf16[3,3,128,128]{3,2,1,0:T(8,128)(2,1)}, u32[]{:S(2)}) copy-start(bf16[3,3,128,128]{3,2,1,0:T(8,128)(2,1)} %param.13) | copy-start | bytes 884740
  7.2 128.4 %all-reduce.11.cloned.1.call-start = ((), (), s32[]{:S(2)}) async-start(), calls=%async_computation.1 | async-start | bytes 2359296 | tf_op jit(solution)/shard_map/psum | solution.py:173
  9.1 7.5 %copy-start.13 = (bf16[1,12,6,256]{3,2,1,0:T(8,128)(2,1)S(1)}, bf16[1,12,6,256]{3,2,1,0:T(8,128)(2,1)}, u32[]{:S(2)}) copy-start(bf16[1,12,6,256]{3,2,1,0:T(8,128)(2,1)} %param.17) | copy-start | bytes 110596
  9.1 7.5 %copy-start.14 = (bf16[12,128]{1,0:T(8,128)(2,1)S(1)}, bf16[12,128]{1,0:T(8,128)(2,1)}, u32[]{:S(2)}) copy-start(bf16[12,128]{1,0:T(8,128)(2,1)} %param.16) | copy-start | bytes 9220
  9.1 7.8 %copy-start.9 = (bf16[1,128,128]{2,1,0:T(8,128)(2,1)S(1)}, bf16[1,128,128]{2,1,0:T(8,128)(2,1)}, u32[]{:S(2)}) copy-start(bf16[1,128,128]{2,1,0:T(8,128)(2,1)} %param.15) | copy-start | bytes 98308
  11.1 16.9 %copy-start.4 = (bf16[128,6,256]{0,2,1:T(8,128)(2,1)}, bf16[128,6,256]{0,2,1:T(8,128)(2,1)S(1)}, u32[]{:S(2)}) copy-start(bf16[128,6,256]{0,2,1:T(8,128)(2,1)S(1)} %get-tuple-element.52) | copy-start | bytes 1179652
  11.1 16.9 %collective-permute-start = (bf16[1,128,1,256]{1,3,2,0:T(8,128)(2,1)S(1)}, bf16[1,128,1,256]{1,3,2,0:T(8,128)(2,1)S(1)}, u32[]{:S(2)}, u32[]{:S(2)}) collective-permute-start(bf16[1,128,1,256]{1,3,2,0:T(8,128)(2,1)S(1)} %get-tuple-element.46), channel_id=1, source_target_pairs={{0,2},{2,4},{4,6},{6,8},{8,10},{10,12},{12,14},{14,16},{16,18},{18... | collective-permute-start | bytes 196616 | tf_op jit(solution)/shard_map/ppermute | solution.py:19
  11.6 16.4 %collective-permute-start.1 = (bf16[1,128,1,256]{1,3,2,0:T(8,128)(2,1)S(1)}, bf16[1,128,1,256]{1,3,2,0:T(8,128)(2,1)S(1)}, u32[]{:S(2)}, u32[]{:S(2)}) collective-permute-start(bf16[1,128,1,256]{1,3,2,0:T(8,128)(2,1)S(1)} %get-tuple-element.47), channel_id=1, source_target_pairs={{2,0},{4,2},{6,4},{8,6},{10,8},{12,10},{14,12},{16,14},{18,16},{20... | collective-permute-start | bytes 196616 | tf_op jit(solution)/shard_map/ppermute | solution.py:22
  18.9 12.7 %collective-permute-start.4 = (bf16[1,128,2,256]{1,3,2,0:T(8,128)(2,1)}, bf16[1,128,2,256]{1,3,2,0:T(8,128)(2,1)S(1)}, u32[]{:S(2)}, u32[]{:S(2)}) collective-permute-start(bf16[1,128,2,256]{1,3,2,0:T(8,128)(2,1)} %get-tuple-element.48), channel_id=1, source_target_pairs={{0,2},{2,4},{4,6},{6,8},{8,10},{10,12},{12,14},{14,16},{16,18},{18... | collective-permute-start | bytes 393224 | tf_op jit(solution)/shard_map/ppermute | solution.py:19
  18.9 12.7 %collective-permute-start.5 = (bf16[1,128,2,256]{1,3,2,0:T(8,128)(2,1)}, bf16[1,128,2,256]{1,3,2,0:T(8,128)(2,1)S(1)}, u32[]{:S(2)}, u32[]{:S(2)}) collective-permute-start(bf16[1,128,2,256]{1,3,2,0:T(8,128)(2,1)} %get-tuple-element.49), channel_id=1, source_target_pairs={{2,0},{4,2},{6,4},{8,6},{10,8},{12,10},{14,12},{16,14},{18,16},{20... | collective-permute-start | bytes 393224 | tf_op jit(solution)/shard_map/ppermute | solution.py:22
  28.0 0.6 copy-start.10
  28.6 0.7 copy-start.18
  34.0 1.0 copy-start.15
  42.2 1.0 copy-start.5
  43.5 9.6 %copy-start.11 = (bf16[1,128,1,256]{1,3,2,0:T(8,128)(2,1)S(1)}, bf16[1,128,1,256]{1,3,2,0:T(8,128)(2,1)}, u32[]{:S(2)}) copy-start(bf16[1,128,1,256]{1,3,2,0:T(8,128)(2,1)} %copy-done.10) | copy-start | bytes 196612
  44.1 10.5 %collective-permute-start.6 = (bf16[1,128,1,256]{1,3,2,0:T(8,128)(2,1)S(1)}, bf16[1,128,1,256]{1,3,2,0:T(8,128)(2,1)S(1)}, u32[]{:S(2)}, u32[]{:S(2)}) collective-permute-start(bf16[1,128,1,256]{1,3,2,0:T(8,128)(2,1)S(1)} %get-tuple-element.42), channel_id=1, source_target_pairs={{0,2},{2,4},{4,6},{6,8},{8,10},{10,12},{12,14},{14,16},{16,18},{18... | collective-permute-start | bytes 196616 | tf_op jit(solution)/shard_map/ppermute | solution.py:19
  44.2 10.4 %collective-permute-start.7 = (bf16[1,128,1,256]{1,3,2,0:T(8,128)(2,1)S(1)}, bf16[1,128,1,256]{1,3,2,0:T(8,128)(2,1)S(1)}, u32[]{:S(2)}, u32[]{:S(2)}) collective-permute-start(bf16[1,128,1,256]{1,3,2,0:T(8,128)(2,1)S(1)} %get-tuple-element.43), channel_id=1, source_target_pairs={{2,0},{4,2},{6,4},{8,6},{10,8},{12,10},{14,12},{16,14},{18,16},{20... | collective-permute-start | bytes 196616 | tf_op jit(solution)/shard_map/ppermute | solution.py:22
  48.6 8.8 %collective-permute-start.2 = (bf16[1,128,2,256]{1,3,2,0:T(8,128)(2,1)S(1)}, bf16[1,128,2,256]{1,3,2,0:T(8,128)(2,1)S(1)}, u32[]{:S(2)}, u32[]{:S(2)}) collective-permute-start(bf16[1,128,2,256]{1,3,2,0:T(8,128)(2,1)S(1)} %get-tuple-element.44), channel_id=1, source_target_pairs={{0,2},{2,4},{4,6},{6,8},{8,10},{10,12},{12,14},{14,16},{16,18},{18... | collective-permute-start | bytes 393224 | tf_op jit(solution)/shard_map/ppermute | solution.py:19
  48.6 8.8 %collective-permute-start.3 = (bf16[1,128,2,256]{1,3,2,0:T(8,128)(2,1)S(1)}, bf16[1,128,2,256]{1,3,2,0:T(8,128)(2,1)S(1)}, u32[]{:S(2)}, u32[]{:S(2)}) collective-permute-start(bf16[1,128,2,256]{1,3,2,0:T(8,128)(2,1)S(1)} %get-tuple-element.45), channel_id=1, source_target_pairs={{2,0},{4,2},{6,4},{8,6},{10,8},{12,10},{14,12},{16,14},{18,16},{20... | collective-permute-start | bytes 393224 | tf_op jit(solution)/shard_map/ppermute | solution.py:22
  60.3 0.8 copy-start.7
  61.1 1.3 copy-start.3
  61.2 1.6 copy-start.1
  61.2 1.8 copy-start.2
  62.1 164.2 %all-reduce.9.cloned.1.call-start = ((), (), s32[]{:S(2)}) async-start(), calls=%async_computation | async-start | bytes 2490368 | tf_op jit(solution)/shard_map/psum | solution.py:138
  63.0 0.7 copy-start.17
  132.2 1.0 copy-start.16
  136.8 8.6 %copy-start.8 = (bf16[2,128,128]{2,1,0:T(8,128)(2,1)S(1)}, bf16[2,128,128]{2,1,0:T(8,128)(2,1)}, u32[]{:S(2)}) copy-start(bf16[2,128,128]{2,1,0:T(8,128)(2,1)} %all_gather.7) | copy-start | bytes 196612
  226.3 2.0 copy-start.6
  226.3 2.9 %copy-start.12 = (f32[128,128]{1,0:T(8,128)S(1)}, f32[128,128]{1,0:T(8,128)}, u32[]{:S(2)}) copy-start(f32[128,128]{1,0:T(8,128)} %get-tuple-element.26) | copy-start | bytes 196612
Sparse Core Ops, SparseCore 0:
  62.2 42.9 all-reduce.10
  135.7 90.4 all-reduce.8
